TPU v7x, 32 devices: a whole 2x2x4 slice. The times are simulated.
32 devices in a mesh: grid: 8 (over z, y), snap: 4 (over x, core).
Axes of the slice: x: 2, y: 2, z: 4, core: 2. Of those that a mesh axis runs over, the one named last changes fastest.
Arguments:
- fields: bfloat16 [49152, 1024], P('grid', 'snap'), may hold values from -40 to 40
- start_local: float32 [1024, 128], P('snap'), may hold values from -6 to 6
- start_pair: float32 [2, 256, 128], replicated, may hold values from -6 to 6
- start_root: float32 [256, 128], replicated, may hold values from -6 to 6
Outputs:
- modes: bfloat16 [49152, 128], P(('grid', 'snap'))
All inputs are finite; a program needn't handle non-finite values.
Results may differ from a plain program's by a relative error of at most 0.0055.
Values may be sent and summed in bfloat16 or wider, within the bound.
No kernel may reach another device: no remote copies, remote signals or barrier semaphores. Data moves between devices by JAX's collectives and lax.ppermute only.
A program may use at most 64 MiB of HBM per device.

v0:
```python
import jax
import jax.numpy as jnp
from jax import lax
from jax.sharding import PartitionSpec as P

POWER = 2
NEWTON = 8


def from_partner(value, axis, bit):
    mask = 2**bit
    pairs = [(source, source ^ mask) for source in range(lax.axis_size(axis))]
    return lax.ppermute(value, axis, pairs)


def polar_basis(gram_matrix, initial):
    current = initial
    for power_step in range(POWER):
        product = jnp.dot(gram_matrix, current, precision=lax.Precision.HIGHEST)
        iterate = product / jnp.sqrt(jnp.sum(product * product) + 1e-06)
        for newton_step in range(NEWTON):
            inner_gram = jnp.dot(iterate.T, iterate, precision=lax.Precision.HIGHEST)
            iterate = 1.5 * iterate - 0.5 * jnp.dot(
                iterate, inner_gram, precision=lax.Precision.HIGHEST
            )
        current = iterate
    return current


def rotate(joined, rotation):
    return jnp.dot(
        joined, rotation.astype(jnp.bfloat16), preferred_element_type=jnp.float32
    ).astype(jnp.bfloat16)


def on_device(fields, start_local, start_pair, start_root):
    local_rows = fields.shape[0]
    inverse_count = 1.0 / (local_rows * lax.axis_size("grid"))
    partial_gram = jnp.dot(fields.T, fields, preferred_element_type=jnp.float32)
    gram_sum = lax.psum(partial_gram, "grid") * inverse_count
    rotation = polar_basis(gram_sum, start_local)
    leaf_field = rotate(fields, rotation)
    position = lax.axis_index("snap")
    low_bit = position % 2
    high_bit = position // 2
    node_start = lax.dynamic_index_in_dim(start_pair, high_bit, 0, keepdims=False)
    quarter = local_rows // 4
    partner = from_partner(leaf_field, "snap", 0)
    lower_part = jnp.where(low_bit == 0, leaf_field, partner)
    upper_part = jnp.where(low_bit == 0, partner, leaf_field)
    joined = jnp.concatenate([lower_part, upper_part], axis=1)
    partial_gram = jnp.dot(joined.T, joined, preferred_element_type=jnp.float32)
    gram_sum = lax.psum(partial_gram, "grid") * inverse_count
    branch = rotate(joined, polar_basis(gram_sum, node_start))
    partner = from_partner(branch, "snap", 1)
    lower_part = jnp.where(high_bit == 0, branch, partner)
    upper_part = jnp.where(high_bit == 0, partner, branch)
    joined = jnp.concatenate([lower_part, upper_part], axis=1)
    partial_gram = jnp.dot(joined.T, joined, preferred_element_type=jnp.float32)
    gram_sum = lax.psum(partial_gram, "grid") * inverse_count
    rotation = polar_basis(gram_sum, start_root)
    own_rows = lax.dynamic_slice_in_dim(joined, position * quarter, quarter, 0)
    return rotate(own_rows, rotation)


def solution(mesh):
    in_specs = (P("grid", "snap"), P("snap", None), P(), P())
    out_specs = P(("grid", "snap"), None)
    return jax.shard_map(
        on_device, mesh=mesh, in_specs=in_specs, out_specs=out_specs, check_vma=False
    )
```

profile of v0, /device:TPU:0, one launch (start us, length us, event | category | flops | bytes accessed | tf_op | source)
XLA Modules:
  0.0 331.3 jit_solution(1341703258600756548)
XLA Ops:
  6.5 1.9 copy-done
  8.4 1.7 fusion.94
  10.2 74.2 %all-reduce.4.cloned.1.call-done = f32[256,256]{1,0:T(8,128)} async-done(((f32[256,256]{1,0:T(8,128)}), f32[256,256]{1,0:T(8,128)}) %all-reduce.4.cloned.1.call-update) | async-done | bytes 262160 | tf_op jit(solution)/shard_map/psum | solution.py:40
  84.4 1.9 multiply_reduce_fusion.5
  87.1 0.4 fusion.76
  88.4 0.4 fusion.96
  89.7 0.4 fusion.98
  90.4 0.4 fusion.99
  91.0 0.4 fusion.100
  91.7 0.4 fusion.101
  92.4 1.0 multiply_reduce_fusion.4
  94.0 0.4 fusion.77
  94.7 0.4 fusion.102
  95.4 0.4 fusion.103
  96.7 0.4 fusion.105
  97.4 0.4 fusion.106
  98.0 0.4 fusion.107
  98.7 0.4 fusion.108
  99.3 2.3 fusion
  101.7 3.7 %collective-permute-done = bf16[6144,128]{0,1:T(8,128)(2,1)} collective-permute-done((bf16[6144,128]{0,1:T(8,128)(2,1)}, bf16[6144,128]{0,1:T(8,128)(2,1)}, u32[]{:S(2)}, u32[]{:S(2)}) %collective-permute-start) | collective-permute-done | bytes 1572896 | tf_op jit(solution)/shard_map/ppermute | solution.py:13
  105.4 2.1 broadcast_select_fusion.1
  107.5 1.1 copy-done.5
  108.7 0.5 copy-done.7
  109.2 1.7 fusion.2
  111.1 70.1 %all-reduce.6.cloned.1.call-done = f32[256,256]{1,0:T(8,128)} async-done(((f32[256,256]{1,0:T(8,128)}), f32[256,256]{1,0:T(8,128)}) %all-reduce.6.cloned.1.call-update) | async-done | bytes 262160 | tf_op jit(solution)/shard_map/psum | solution.py:53
  181.3 1.9 multiply_reduce_fusion.3
  183.9 0.4 fusion.78
  184.5 0.4 fusion.109
  185.2 0.4 fusion.110
  185.9 0.4 fusion.111
  186.5 0.4 fusion.112
  187.2 0.4 fusion.113
  187.9 0.4 fusion.114
  189.2 1.0 multiply_reduce_fusion.2
  190.9 0.4 fusion.79
  192.2 0.4 fusion.117
  193.5 0.4 fusion.119
  194.9 0.4 fusion.121
  195.5 0.4 fusion.122
  196.2 1.8 convolution_convert_fusion
  198.0 1.5 collective-permute-start.1
  199.4 33.1 %collective-permute-done.1 = bf16[6144,128]{0,1:T(8,128)(2,1)} collective-permute-done((bf16[6144,128]{0,1:T(8,128)(2,1)}, bf16[6144,128]{0,1:T(8,128)(2,1)}, u32[]{:S(2)}, u32[]{:S(2)}) %collective-permute-start.1) | collective-permute-done | bytes 1572896 | tf_op jit(solution)/shard_map/ppermute | solution.py:13
  232.6 2.1 broadcast_select_fusion.3
  234.7 1.1 copy-done.1
  235.8 0.5 copy-done.3
  236.3 1.7 fusion.1
  238.1 70.4 %all-reduce.8.cloned.1.call-done = f32[256,256]{1,0:T(8,128)} async-done(((f32[256,256]{1,0:T(8,128)}), f32[256,256]{1,0:T(8,128)}) %all-reduce.8.cloned.1.call-update) | async-done | bytes 262160 | tf_op jit(solution)/shard_map/psum | solution.py:60
  308.4 1.9 multiply_reduce_fusion.1
  311.1 0.6 fusion.80
  311.9 0.4 fusion.123
  312.6 0.4 fusion.124
  313.3 0.4 fusion.125
  313.9 0.4 fusion.126
  315.3 0.4 fusion.128
  315.9 0.4 fusion.129
  316.6 1.0 multiply_reduce_fusion
  318.3 0.4 fusion.81
  318.9 0.4 fusion.130
  319.6 0.4 fusion.131
  320.3 0.4 fusion.132
  320.9 0.4 fusion.133
  321.6 0.4 fusion.134
  322.2 0.4 fusion.135
  323.6 1.2 convolution_convert_fusion.2
  (89 shorter events, 16.4 us)
Async XLA Ops:
  6.5 1.9 copy-start
  6.5 77.9 %copy-start.12 = (f32[256,128]{1,0:T(8,128)S(1)}, f32[256,128]{1,0:T(8,128)}, u32[]{:S(2)}) copy-start(f32[256,128]{1,0:T(8,128)} %param.5) | copy-start | bytes 393220
  6.5 77.9 %all-reduce.4.cloned.1.call-start = ((), (), s32[]{:S(2)}) async-start(), calls=%async_computation | async-start | bytes 524288 | tf_op jit(solution)/shard_map/psum | solution.py:40
  10.2 171.1 %all-reduce.6.cloned.1.call-start = ((), (), s32[]{:S(2)}) async-start(), calls=%async_computation.1 | async-start | bytes 524288 | tf_op jit(solution)/shard_map/psum | solution.py:53
  89.1 3.3 %copy-start.10 = (f32[256,256]{1,0:T(8,128)S(1)}, f32[256,256]{1,0:T(8,128)}, u32[]{:S(2)}) copy-start(f32[256,256]{1,0:T(8,128)} %all-reduce.4.cloned.1.call-done) | copy-start | bytes 786436
  101.7 3.8 %collective-permute-start = (bf16[6144,128]{0,1:T(8,128)(2,1)}, bf16[6144,128]{0,1:T(8,128)(2,1)}, u32[]{:S(2)}, u32[]{:S(2)}) collective-permute-start(bf16[6144,128]{0,1:T(8,128)(2,1)} %fusion), channel_id=1, source_target_pairs={{0,1},{1,0},{2,3},{3,2},{4,5},{5,4},{6,7},{7,6},{8,9},{9,8},{10,11... | collective-permute-start | bytes 4718600 | tf_op jit(solution)/shard_map/ppermute | solution.py:13
  107.5 1.2 copy-start.5
  107.5 1.6 copy-start.7
  109.1 72.1 %copy-start.14 = (f32[2,256,128]{2,1,0:T(8,128)S(1)}, f32[2,256,128]{2,1,0:T(8,128)}, u32[]{:S(2)}) copy-start(f32[2,256,128]{2,1,0:T(8,128)} %param.6) | copy-start | bytes 786436
  110.9 197.5 %all-reduce.8.cloned.1.call-start = ((), (), s32[]{:S(2)}) async-start(), calls=%async_computation.2 | async-start | bytes 524288 | tf_op jit(solution)/shard_map/psum | solution.py:60
  185.9 3.3 %copy-start.11 = (f32[256,256]{1,0:T(8,128)S(1)}, f32[256,256]{1,0:T(8,128)}, u32[]{:S(2)}) copy-start(f32[256,256]{1,0:T(8,128)} %all-reduce.6.cloned.1.call-done) | copy-start | bytes 786436
  192.9 3.3 %copy-start.6 = (bf16[6144,128]{0,1:T(8,128)(2,1)S(1)}, bf16[6144,128]{0,1:T(8,128)(2,1)}, u32[]{:S(2)}) copy-start(bf16[6144,128]{0,1:T(8,128)(2,1)} %copy-done.5) | copy-start | bytes 4718596
  192.9 3.3 %copy-start.8 = (bf16[6144,128]{0,1:T(8,128)(2,1)S(1)}, bf16[6144,128]{0,1:T(8,128)(2,1)}, u32[]{:S(2)}) copy-start(bf16[6144,128]{0,1:T(8,128)(2,1)} %copy-done.7) | copy-start | bytes 4718596
  198.0 34.6 %collective-permute-start.1 = (bf16[6144,128]{0,1:T(8,128)(2,1)}, bf16[6144,128]{0,1:T(8,128)(2,1)}, u32[]{:S(2)}, u32[]{:S(2)}) collective-permute-start(bf16[6144,128]{0,1:T(8,128)(2,1)} %convolution_convert_fusion), channel_id=1, source_target_pairs={{0,2},{1,3},{2,0},{3,1},{4,6},{5,7},{6,4},{7,5},{8,10},{9,11},{10,... | collective-permute-start | bytes 4718600 | tf_op jit(solution)/shard_map/ppermute | solution.py:13
  234.7 1.1 copy-start.1
  234.7 1.6 copy-start.3
  236.3 72.1 %copy-start.13 = (f32[256,128]{1,0:T(8,128)S(1)}, f32[256,128]{1,0:T(8,128)}, u32[]{:S(2)}) copy-start(f32[256,128]{1,0:T(8,128)} %param.7) | copy-start | bytes 393220
  313.3 3.3 %copy-start.9 = (f32[256,256]{1,0:T(8,128)S(1)}, f32[256,256]{1,0:T(8,128)}, u32[]{:S(2)}) copy-start(f32[256,256]{1,0:T(8,128)} %all-reduce.8.cloned.1.call-done) | copy-start | bytes 786436
  320.2 3.3 %copy-start.2 = (bf16[6144,128]{0,1:T(8,128)(2,1)S(1)}, bf16[6144,128]{0,1:T(8,128)(2,1)}, u32[]{:S(2)}) copy-start(bf16[6144,128]{0,1:T(8,128)(2,1)} %copy-done.1) | copy-start | bytes 4718596
  320.3 3.3 %copy-start.4 = (bf16[6144,128]{0,1:T(8,128)(2,1)S(1)}, bf16[6144,128]{0,1:T(8,128)(2,1)}, u32[]{:S(2)}) copy-start(bf16[6144,128]{0,1:T(8,128)(2,1)} %copy-done.3) | copy-start | bytes 4718596
Sparse Core Ops, SparseCore 0:
  10.7 73.7 all-reduce.3
  111.0 70.1 all-reduce.5
  238.2 70.1 all-reduce.7
where the time goes:
time: 332 us; the launch traced here: 331 us
  waiting for transfers between devices  252 us (76%)
  matrix products  50.5 us (15%)
  between operations  18 us (5%)
  local copies, waits for them, and re-layouts  5.19 us (2%)
  other arithmetic  4.18 us (1%)
    psum x3, waiting for transfers between devices, on_device(): gram_sum = lax.psum(partial_gram, 'grid') * inverse_count  215 us
    ppermute x2, waiting for transfers between devices, from_partner(): return lax.ppermute(value, axis, pairs)  36.9 us
    dot_general x48, matrix products, polar_basis(): inner_gram = jnp.dot(iterate.T, iterate, precision=lax.Precision.HIGHEST)  18.8 us
    dot_general x48, matrix products, polar_basis(): jnp.dot(iterate, inner_gram, precision=lax.Precision.HIGHEST)  12.6 us
    dot_general x6, matrix products, polar_basis(): product = jnp.dot(gram_matrix, current, precision=lax.Precision.HIGHEST)  8.74 us
  transfers between devices with their start and end apart: 5, of which 5 were waited for; matrix products, arithmetic and copies ran while one was open for 0% of the time, Pallas kernels for 0%

commit v1 on v0

--- a/solution.py
+++ b/solution.py
@@ -5,6 +5,11 @@
 
 POWER = 2
 NEWTON = 8
+
+
+def add_all(x, name):
+    terms = lax.all_gather(x, name)
+    return jnp.sum(terms, axis=0)
 
 
 def from_partner(value, axis, bit):
@@ -37,7 +42,7 @@
     local_rows = fields.shape[0]
     inverse_count = 1.0 / (local_rows * lax.axis_size("grid"))
     partial_gram = jnp.dot(fields.T, fields, preferred_element_type=jnp.float32)
-    gram_sum = lax.psum(partial_gram, "grid") * inverse_count
+    gram_sum = add_all(partial_gram, "grid") * inverse_count
     rotation = polar_basis(gram_sum, start_local)
     leaf_field = rotate(fields, rotation)
     position = lax.axis_index("snap")

time: 332 us -> 312 us (0.940)
  waiting for transfers between devices: 252 us -> 229 us
    psum x3 -> x2, waiting for transfers between devices: 215 us -> 140 us  [on_device(): gram_sum = lax.psum(partial_gram, 'grid') * inverse_count]
    all_gather x0 -> x1, waiting for transfers between devices: none -> 51.9 us  [add_all(): terms = lax.all_gather(x, name)]
where the time goes in v1:
time: 312 us
  waiting for transfers between devices  229 us (73%)
  matrix products  52.3 us (17%)
  between operations  18.1 us (6%)
  other arithmetic  5.93 us (2%)
  local copies, waits for them, and re-layouts  5.19 us (2%)
    psum x2, waiting for transfers between devices, on_device(): gram_sum = lax.psum(partial_gram, 'grid') * inverse_count  140 us
    all_gather x1, waiting for transfers between devices, add_all(): terms = lax.all_gather(x, name)  51.9 us
    ppermute x2, waiting for transfers between devices, from_partner(): return lax.ppermute(value, axis, pairs)  36.9 us
    dot_general x48, matrix products, polar_basis(): inner_gram = jnp.dot(iterate.T, iterate, precision=lax.Precision.HIGHEST)  19.8 us
    dot_general x48, matrix products, polar_basis(): jnp.dot(iterate, inner_gram, precision=lax.Precision.HIGHEST)  13.6 us
    dot_general x6, matrix products, polar_basis(): product = jnp.dot(gram_matrix, current, precision=lax.Precision.HIGHEST)  8.52 us
  transfers between devices with their start and end apart: 5, of which 5 were waited for; matrix products, arithmetic and copies ran while one was open for 0% of the time, Pallas kernels for 0%

profile of v1, /device:TPU:0, one launch (start us, length us, event | category | flops | bytes accessed | tf_op | source)
XLA Modules:
  0.0 311.8 jit_solution(10444998393201040242)
XLA Ops:
  6.5 1.9 copy-done
  8.4 1.7 fusion.94
  10.2 51.9 %all-gather.3.cloned.1.call-done = f32[2048,256]{1,0:T(8,128)} async-done(((f32[256,256]{1,0:T(8,128)}), f32[2048,256]{1,0:T(8,128)}) %all-gather.3.cloned.1.call-update) | async-done | bytes 2097168 | tf_op jit(solution)/shard_map/all_gather | solution.py:11
  62.1 1.8 reduce_sum.63
  63.9 1.7 multiply_reduce_fusion.5
  66.3 1.4 fusion.76
  67.7 1.2 fusion.3
  69.6 0.4 fusion.96
  71.0 0.4 fusion.98
  71.6 0.4 fusion.99
  72.9 0.4 fusion.101
  73.6 1.0 multiply_reduce_fusion.4
  75.3 0.4 fusion.77
  75.9 0.4 fusion.102
  76.6 0.4 fusion.103
  77.9 0.4 fusion.105
  78.6 0.4 fusion.106
  79.2 0.4 fusion.107
  79.9 0.4 fusion.108
  80.6 2.3 fusion
  82.9 3.7 %collective-permute-done = bf16[6144,128]{0,1:T(8,128)(2,1)} collective-permute-done((bf16[6144,128]{0,1:T(8,128)(2,1)}, bf16[6144,128]{0,1:T(8,128)(2,1)}, u32[]{:S(2)}, u32[]{:S(2)}) %collective-permute-start) | collective-permute-done | bytes 1572896 | tf_op jit(solution)/shard_map/ppermute | solution.py:18
  86.6 2.1 broadcast_select_fusion.1
  88.8 1.1 copy-done.5
  89.9 0.5 copy-done.7
  90.4 1.7 fusion.2
  92.4 69.4 %all-reduce.3.cloned.1.call-done = f32[256,256]{1,0:T(8,128)} async-done(((f32[256,256]{1,0:T(8,128)}), f32[256,256]{1,0:T(8,128)}) %all-reduce.3.cloned.1.call-update) | async-done | bytes 262160 | tf_op jit(solution)/shard_map/psum | solution.py:58
  161.8 1.9 multiply_reduce_fusion.3
  164.4 0.4 fusion.78
  165.8 0.4 fusion.110
  167.1 0.4 fusion.112
  167.8 0.4 fusion.113
  169.1 0.4 fusion.115
  169.8 1.0 multiply_reduce_fusion.2
  171.4 0.4 fusion.79
  172.1 0.4 fusion.116
  172.8 0.4 fusion.117
  173.4 0.4 fusion.118
  174.8 0.4 fusion.120
  175.4 0.4 fusion.121
  176.1 0.4 fusion.122
  176.8 1.8 convolution_convert_fusion
  178.5 1.5 collective-permute-start.1
  180.0 33.1 %collective-permute-done.1 = bf16[6144,128]{0,1:T(8,128)(2,1)} collective-permute-done((bf16[6144,128]{0,1:T(8,128)(2,1)}, bf16[6144,128]{0,1:T(8,128)(2,1)}, u32[]{:S(2)}, u32[]{:S(2)}) %collective-permute-start.1) | collective-permute-done | bytes 1572896 | tf_op jit(solution)/shard_map/ppermute | solution.py:18
  213.1 2.1 broadcast_select_fusion.3
  215.3 1.1 copy-done.1
  216.4 0.5 copy-done.3
  216.9 1.7 fusion.1
  218.6 70.3 %all-reduce.5.cloned.1.call-done = f32[256,256]{1,0:T(8,128)} async-done(((f32[256,256]{1,0:T(8,128)}), f32[256,256]{1,0:T(8,128)}) %all-reduce.5.cloned.1.call-update) | async-done | bytes 262160 | tf_op jit(solution)/shard_map/psum | solution.py:65
  289.0 1.9 multiply_reduce_fusion.1
  291.6 0.6 fusion.80
  292.5 0.4 fusion.123
  293.1 0.4 fusion.124
  294.5 0.4 fusion.126
  295.1 0.4 fusion.127
  296.4 0.4 fusion.129
  297.1 1.0 multiply_reduce_fusion
  298.8 0.4 fusion.81
  299.4 0.4 fusion.130
  300.1 0.4 fusion.131
  300.8 0.4 fusion.132
  302.1 0.4 fusion.134
  302.8 0.4 fusion.135
  303.4 0.4 fusion.136
  304.1 1.2 convolution_convert_fusion.2
  (88 shorter events, 16.9 us)
Async XLA Ops:
  6.5 1.9 copy-start
  6.5 55.6 %all-gather.3.cloned.1.call-start = ((), (), s32[]{:S(2)}) async-start(), calls=%async_computation.2 | async-start | bytes 2359296 | tf_op jit(solution)/shard_map/all_gather | solution.py:11
  10.1 53.8 %copy-start.11 = (f32[256,128]{1,0:T(8,128)S(1)}, f32[256,128]{1,0:T(8,128)}, u32[]{:S(2)}) copy-start(f32[256,128]{1,0:T(8,128)} %param.5) | copy-start | bytes 393220
  10.2 151.6 %all-reduce.3.cloned.1.call-start = ((), (), s32[]{:S(2)}) async-start(), calls=%async_computation | async-start | bytes 524288 | tf_op jit(solution)/shard_map/psum | solution.py:58
  82.9 3.8 %collective-permute-start = (bf16[6144,128]{0,1:T(8,128)(2,1)}, bf16[6144,128]{0,1:T(8,128)(2,1)}, u32[]{:S(2)}, u32[]{:S(2)}) collective-permute-start(bf16[6144,128]{0,1:T(8,128)(2,1)} %fusion), channel_id=1, source_target_pairs={{0,1},{1,0},{2,3},{3,2},{4,5},{5,4},{6,7},{7,6},{8,9},{9,8},{10,11... | collective-permute-start | bytes 4718600 | tf_op jit(solution)/shard_map/ppermute | solution.py:18
  88.7 1.2 copy-start.5
  88.7 1.6 copy-start.7
  90.4 71.4 %copy-start.13 = (f32[2,256,128]{2,1,0:T(8,128)S(1)}, f32[2,256,128]{2,1,0:T(8,128)}, u32[]{:S(2)}) copy-start(f32[2,256,128]{2,1,0:T(8,128)} %param.6) | copy-start | bytes 786436
  92.1 196.8 %all-reduce.5.cloned.1.call-start = ((), (), s32[]{:S(2)}) async-start(), calls=%async_computation.1 | async-start | bytes 524288 | tf_op jit(solution)/shard_map/psum | solution.py:65
  166.4 3.3 %copy-start.10 = (f32[256,256]{1,0:T(8,128)S(1)}, f32[256,256]{1,0:T(8,128)}, u32[]{:S(2)}) copy-start(f32[256,256]{1,0:T(8,128)} %all-reduce.3.cloned.1.call-done) | copy-start | bytes 786436
  173.4 3.3 %copy-start.6 = (bf16[6144,128]{0,1:T(8,128)(2,1)S(1)}, bf16[6144,128]{0,1:T(8,128)(2,1)}, u32[]{:S(2)}) copy-start(bf16[6144,128]{0,1:T(8,128)(2,1)} %copy-done.5) | copy-start | bytes 4718596
  173.4 3.3 %copy-start.8 = (bf16[6144,128]{0,1:T(8,128)(2,1)S(1)}, bf16[6144,128]{0,1:T(8,128)(2,1)}, u32[]{:S(2)}) copy-start(bf16[6144,128]{0,1:T(8,128)(2,1)} %copy-done.7) | copy-start | bytes 4718596
  178.5 34.6 %collective-permute-start.1 = (bf16[6144,128]{0,1:T(8,128)(2,1)}, bf16[6144,128]{0,1:T(8,128)(2,1)}, u32[]{:S(2)}, u32[]{:S(2)}) collective-permute-start(bf16[6144,128]{0,1:T(8,128)(2,1)} %convolution_convert_fusion), channel_id=1, source_target_pairs={{0,2},{1,3},{2,0},{3,1},{4,6},{5,7},{6,4},{7,5},{8,10},{9,11},{10,... | collective-permute-start | bytes 4718600 | tf_op jit(solution)/shard_map/ppermute | solution.py:18
  215.2 1.2 copy-start.1
  215.2 1.6 copy-start.3
  216.9 72.1 %copy-start.12 = (f32[256,128]{1,0:T(8,128)S(1)}, f32[256,128]{1,0:T(8,128)}, u32[]{:S(2)}) copy-start(f32[256,128]{1,0:T(8,128)} %param.7) | copy-start | bytes 393220
  293.8 3.3 %copy-start.9 = (f32[256,256]{1,0:T(8,128)S(1)}, f32[256,256]{1,0:T(8,128)}, u32[]{:S(2)}) copy-start(f32[256,256]{1,0:T(8,128)} %all-reduce.5.cloned.1.call-done) | copy-start | bytes 786436
  300.8 3.3 %copy-start.2 = (bf16[6144,128]{0,1:T(8,128)(2,1)S(1)}, bf16[6144,128]{0,1:T(8,128)(2,1)}, u32[]{:S(2)}) copy-start(bf16[6144,128]{0,1:T(8,128)(2,1)} %copy-done.1) | copy-start | bytes 4718596
  300.8 3.3 %copy-start.4 = (bf16[6144,128]{0,1:T(8,128)(2,1)S(1)}, bf16[6144,128]{0,1:T(8,128)(2,1)}, u32[]{:S(2)}) copy-start(bf16[6144,128]{0,1:T(8,128)(2,1)} %copy-done.3) | copy-start | bytes 4718596
Sparse Core Ops, SparseCore 0:
  10.3 51.7 all-gather.2
  92.3 69.5 all-reduce.2
  218.7 70.1 all-reduce.4
